TPU v7x, 32 devices: a whole 2x2x4 slice. The times are simulated.
32 devices in a mesh: space: 16 (over z, y, core), grp: 2 (over x).
Axes of the slice: x: 2, y: 2, z: 4, core: 2. Of those that a mesh axis runs over, the one named last changes fastest.
Arguments:
- diag_blocks: float32 [16, 2, 128, 128], P('space', 'grp'), may hold values from -0.4 to 0.4
- x_coupling: float32 [16, 2, 128, 128], P('space', 'grp'), may hold values from -0.35 to 0.35
- y_coupling: float32 [16, 2, 128, 128], P('space', 'grp'), may hold values from -0.35 to 0.35
- levels: float32 [16, 2, 128], P('space', 'grp'), may hold values from -2 to 2
- listed: int32 [16, 2, 2], P('space', 'grp'), may hold values 0 or 1
Outputs:
- density_diag: float32 [16, 2, 128, 128], P('space', 'grp')
- density_x: float32 [16, 2, 128, 128], P('space', 'grp')
- density_y: float32 [16, 2, 128, 128], P('space', 'grp')
Inputs may be any that keep to these rules, and one draw needn't show every extreme that they name: listed[i,j,0] keeps the coupling of block (i,j) with (i+1,j), listed[i,j,1] that with (i,j+1).
All inputs are finite; a program needn't handle non-finite values.
Results may differ from a plain program's by a relative error of at most 0.0037.
Values sent between devices are 32-bit elements; how exact they have to be, the bound alone decides.
A program may use at most 64 MiB of HBM per device.

v0:
```python
import functools

import jax
import jax.numpy as jnp
from jax import lax
from jax.experimental import pallas as pl
from jax.experimental.pallas import tpu as pltpu
from jax.sharding import PartitionSpec as P

hubbard = 1.0
MESH = pl.DeviceIdType.MESH
F32 = jnp.float32
BF16 = jnp.bfloat16


def mm(a, b):
    return jnp.dot(a, b, preferred_element_type=F32)


def eye(w):
    return lax.broadcasted_iota(jnp.int32, (w, w), 0) == lax.broadcasted_iota(jnp.int32, (w, w), 1)


def density_columns(w, row0, v1, dk, sx, fb, v3, u, v1f, cols, after_x, arrived):
    n = 5 * w

    def bl(i):
        return slice(i * w, (i + 1) * w)

    d0 = row0[:, bl(0)]
    for k in arrived(range(4)):
        top = jnp.concatenate([d0, row0[:, bl(1 + k)]], axis=1)
        low = jnp.concatenate([v1[bl(1 + k), :], dk[k]], axis=1)
        pair = jnp.concatenate([top, low], axis=0)
        part = mm(pair, pair).astype(BF16)
        sx[bl(0), bl(1 + k)] = part[:w, w:]
        sx[bl(1 + k), bl(0)] = part[w:, :w]
        sx[bl(1 + k), bl(1 + k)] = part[w:, w:]
    sx[bl(0), bl(0)] = mm(row0[...], v1[...]).astype(BF16)
    for half in range(2):
        t = mm(v1[w:, :], row0[:, w * (1 + 2 * half) : w * (3 + 2 * half)])
        for l in (0, 1):
            k = 2 * half + l
            for r in range(4):
                if r != k:
                    sx[bl(1 + r), bl(1 + k)] = t[bl(r), bl(l)].astype(BF16)
    first = mm(row0[...], sx[:, bl(0)])
    v3[bl(0), :] = first
    sx[bl(0), n:] = first.astype(BF16)
    for k in range(4):
        low = jnp.concatenate([v1[bl(1 + k), :], dk[k]], axis=1)
        vec = jnp.concatenate([sx[bl(0), bl(0)], sx[bl(1 + k), bl(0)]], axis=0)
        first = mm(low, vec)
        v3[bl(1 + k), :] = first
        sx[bl(1 + k), n:] = first.astype(BF16)
    total = jnp.zeros((1, 2 * w), F32)
    for c in range(2):
        f = mm(sx[:, :n], sx[:, 2 * w * c : 2 * w * (c + 1)])
        fb[:, 2 * w * c : 2 * w * (c + 1)] = f.astype(BF16)
        total = total + jnp.sum(f * f, axis=0, keepdims=True)
    f = mm(sx[:, :n], sx[:, 4 * w :])
    v5 = f[:, w:]
    f = f[:, :w]
    fb[:, 4 * w :] = f.astype(BF16)
    total = total[:, :w] + total[:, w:] + jnp.sum(f * f, axis=0, keepdims=True)
    squares = jnp.sum(total, axis=1, keepdims=True)
    scale_two = jnp.sqrt(jnp.sqrt(squares + 1e-06))
    scale_one = jnp.sqrt(scale_two)
    al = 1.5 / scale_one
    be = 0.5 / (scale_one * scale_two)
    c1 = -0.75 * al
    c3 = 0.75 * be + 0.25 * al * al * al
    c5 = -0.75 * al * al * be
    c7 = 0.75 * al * be * be
    c9 = -0.25 * be * be * be
    u[...] = (c5 * v1f[...] + c7 * v3[...] + c9 * v5).astype(BF16)
    top = slice(0, 3 * w)
    cols[top, :] = mm(fb[top, :], u[...]) + (c1 * v1f[top, :] + c3 * v3[top, :])
    cols[bl(0), :] = cols[bl(0), :] + jnp.where(eye(w), 0.5, 0.0)
    after_x()
    top = slice(3 * w, n)
    cols[top, :] = mm(fb[top, :], u[...]) + (c1 * v1f[top, :] + c3 * v3[top, :])


def kernel(
    sizes, diag_hbm, x_hbm, y_hbm, lev_hbm, list_hbm, out_ref,
    din, xin, yin, lin, fin, in_sems,
    send1, rd1, rb1, send2, rd2, rc2, rf3,
    row0, v1, dk, sx, fb, v3, u, v1f, cols, rowf,
    send_sems, recv_sems,
):
    nx, ny = sizes
    w = din.shape[0]
    ix = lax.axis_index("space")
    iy = lax.axis_index("grp")
    has = [ix > 0, ix < nx - 1, iy > 0, iy < ny - 1]
    dev = [
        (jnp.maximum(ix - 1, 0), iy),
        (jnp.minimum(ix + 1, nx - 1), iy),
        (ix, jnp.maximum(iy - 1, 0)),
        (ix, jnp.minimum(iy + 1, ny - 1)),
    ]

    def bl(i):
        return slice(i * w, (i + 1) * w)

    barrier = pltpu.get_barrier_semaphore()
    for k in range(4):
        @pl.when(has[k])
        def _():
            pl.semaphore_signal(barrier, inc=1, device_id=dev[k], device_id_type=MESH)

    loads = [
        pltpu.make_async_copy(diag_hbm.at[0, 0], din, in_sems.at[0]),
        pltpu.make_async_copy(x_hbm.at[0, 0], xin, in_sems.at[1]),
        pltpu.make_async_copy(y_hbm.at[0, 0], yin, in_sems.at[2]),
        pltpu.make_async_copy(lev_hbm.at[0], lin, in_sems.at[3]),
        pltpu.make_async_copy(list_hbm.at[0], fin, in_sems.at[4]),
    ]
    for load in loads:
        load.start()
    for k in range(4):
        @pl.when(jnp.logical_not(has[k]))
        def _():
            zero = jnp.zeros((w, w), F32)
            rd1[k] = zero
            rd2[k] = zero
            rc2[k] = zero
            if k % 2 == 0:
                rb1[k // 2] = zero
            else:
                rf3[k // 2] = zero
    for load in loads:
        load.wait()
    one_eye = eye(w)
    flag_x = fin[0, 0].astype(F32) * (ix < nx - 1).astype(F32)
    flag_y = fin[0, 1].astype(F32) * (iy < ny - 1).astype(F32)
    raw = din[...]
    onsite = 0.5 * (raw + raw.T) + jnp.where(one_eye, jnp.broadcast_to(lin[...], (w, w)), 0.0)
    send1[0] = onsite
    send1[1] = xin[...] * flag_x
    send1[2] = yin[...] * flag_y

    count = sum(h.astype(jnp.int32) for h in has)
    pl.semaphore_wait(barrier, count)

    def transfer(src, dst, index_send, index_recv, k):
        return pltpu.make_async_remote_copy(
            src_ref=src, dst_ref=dst, send_sem=send_sems.at[index_send],
            recv_sem=recv_sems.at[index_recv], device_id=dev[k], device_id_type=MESH,
        )

    def diag1(k):
        return transfer(send1.at[0], rd1.at[k ^ 1], k, k ^ 1, k)

    def coup1(k):
        return transfer(send1.at[1 + k // 2], rb1.at[k // 2], 4 + k // 2, 4 + k // 2, k)

    def diag2(k):
        return transfer(send2, rd2.at[k ^ 1], 6 + k, 6 + (k ^ 1), k)

    def coup2(k):
        return transfer(cols1.at[bl(1 + k), :], rc2.at[k ^ 1], 10 + k, 10 + (k ^ 1), k)

    def coup3(k):
        return transfer(cols2.at[bl(1 + k), :], rf3.at[k // 2], 14 + k // 2, 14 + k // 2, k)

    cols1, cols2 = cols.at[0], cols.at[1]

    order = (1, 0, 3, 2)
    for k in order:
        @pl.when(has[k])
        def _():
            if k % 2:
                coup1(k).start()
            diag1(k).start()

    row0[:, bl(0)] = onsite.astype(BF16)
    v1[bl(0), :] = onsite.astype(BF16)
    v1f[bl(0), :] = onsite
    for axis in range(2):
        coup = send1[1 + axis]
        coup_t = coup.T
        row0[:, bl(2 + 2 * axis)] = coup.astype(BF16)
        v1[bl(2 + 2 * axis), :] = coup_t.astype(BF16)
        v1f[bl(2 + 2 * axis), :] = coup_t
    def arrived1(slots):
        for group in ((2, 3), (1, 0)):
            for k in group:
                @pl.when(has[k])
                def _():
                    if k % 2 == 0:
                        coup1(k ^ 1).wait_recv()
                    diag1(k ^ 1).wait_recv()
            for k in group:
                dk[k] = rd1[k].astype(BF16)
                if k % 2 == 0:
                    coup = rb1[k // 2]
                    row0[:, bl(1 + k)] = coup.T.astype(BF16)
                    v1[bl(1 + k), :] = coup.astype(BF16)
                    v1f[bl(1 + k), :] = coup
            yield from group

    onsite_two = []

    def send_x2():
        for k in (1, 0):
            @pl.when(has[k])
            def _():
                coup2(k).start()
        c0 = cols1[bl(0), :]
        two = v1f[bl(0), :] + hubbard * (0.5 * (c0 + c0.T) - jnp.where(one_eye, 0.5, 0.0))
        send2[...] = two
        onsite_two.append(two)
        for k in order:
            @pl.when(has[k])
            def _():
                diag2(k).start()

    density_columns(w, row0, v1, dk, sx, fb, v3, u, v1f, cols1, send_x2, arrived1)

    for k in (3, 2):
        @pl.when(has[k])
        def _():
            coup2(k).start()
    two = onsite_two[0]
    row0[:, bl(0)] = two.astype(BF16)
    v1[bl(0), :] = two.astype(BF16)
    v1f[bl(0), :] = two
    for k in range(4):
        rowf[k] = (v1f[bl(1 + k), :] + 0.5 * hubbard * cols1[bl(1 + k), :]).T

    def arrived2(slots):
        for group in ((2, 3), (1, 0)):
            for k in group:
                @pl.when(has[k])
                def _():
                    coup2(k ^ 1).wait_recv()
                    diag2(k ^ 1).wait_recv()
            for k in group:
                dk[k] = rd2[k].astype(BF16)
                btk = rowf[k] + 0.5 * hubbard * rc2[k]
                row0[:, bl(1 + k)] = btk.astype(BF16)
                bk = btk.T
                v1f[bl(1 + k), :] = bk
                v1[bl(1 + k), :] = bk.astype(BF16)
            yield from group

    def send_x3():
        @pl.when(has[0])
        def _():
            coup3(0).start()

    density_columns(w, row0, v1, dk, sx, fb, v3, u, v1f, cols2, send_x3, arrived2)

    @pl.when(has[2])
    def _():
        coup3(2).start()
    c0 = cols2[bl(0), :]
    out_ref[0] = 0.5 * (c0 + c0.T)
    half_x = 0.5 * cols2[bl(2), :].T
    half_y = 0.5 * cols2[bl(4), :].T
    for k in (3, 1):
        @pl.when(has[k])
        def _():
            coup3(k ^ 1).wait_recv()
    out_ref[1] = half_x + 0.5 * rf3[0]
    out_ref[2] = half_y + 0.5 * rf3[1]
    for k in range(4):
        @pl.when(has[k])
        def _():
            if k % 2:
                coup1(k).wait_send()
            else:
                coup3(k).wait_send()
            diag1(k).wait_send()
            coup2(k).wait_send()
            diag2(k).wait_send()


def write_out(in_ref, od_ref, ox_ref, oy_ref, sems):
    copies = [
        pltpu.make_async_copy(in_ref.at[i], ref.at[0, 0], sems.at[i])
        for i, ref in enumerate((od_ref, ox_ref, oy_ref))
    ]
    for copy in copies:
        copy.start()
    for copy in copies:
        copy.wait()


def per_device(diag_blocks, x_coupling, y_coupling, levels, listed):
    w = diag_blocks.shape[-1]
    n = 5 * w
    sizes = (lax.axis_size("space"), lax.axis_size("grp"))
    block = jax.ShapeDtypeStruct((1, 1, w, w), F32)
    any_spec = pl.BlockSpec(memory_space=pl.ANY)
    vmem_spec = pl.BlockSpec(memory_space=pltpu.VMEM)
    results = pl.pallas_call(
        functools.partial(kernel, sizes),
        out_shape=pltpu.VMEM((3, w, w), F32),
        in_specs=[any_spec] * 5,
        out_specs=vmem_spec,
        scratch_shapes=[
            pltpu.VMEM((w, w), F32),
            pltpu.VMEM((w, w), F32),
            pltpu.VMEM((w, w), F32),
            pltpu.VMEM((1, w), F32),
            pltpu.SMEM((1, 2), jnp.int32),
            pltpu.SemaphoreType.DMA((5,)),
            pltpu.VMEM((3, w, w), F32),
            pltpu.VMEM((4, w, w), F32),
            pltpu.VMEM((2, w, w), F32),
            pltpu.VMEM((w, w), F32),
            pltpu.VMEM((4, w, w), F32),
            pltpu.VMEM((4, w, w), F32),
            pltpu.VMEM((2, w, w), F32),
            pltpu.VMEM((w, n), BF16),
            pltpu.VMEM((n, w), BF16),
            pltpu.VMEM((4, w, w), BF16),
            pltpu.VMEM((n, n + w), BF16),
            pltpu.VMEM((n, n), BF16),
            pltpu.VMEM((n, w), F32),
            pltpu.VMEM((n, w), BF16),
            pltpu.VMEM((n, w), F32),
            pltpu.VMEM((2, n, w), F32),
            pltpu.VMEM((4, w, w), F32),
            pltpu.SemaphoreType.DMA((16,)),
            pltpu.SemaphoreType.DMA((16,)),
        ],
        compiler_params=pltpu.CompilerParams(collective_id=0, has_side_effects=True),
    )(diag_blocks, x_coupling, y_coupling, levels, listed)
    return pl.pallas_call(
        write_out,
        out_shape=(block, block, block),
        in_specs=[vmem_spec],
        out_specs=(any_spec,) * 3,
        scratch_shapes=[pltpu.SemaphoreType.DMA((3,))],
    )(pltpu.with_memory_space_constraint(results, pltpu.VMEM))


def solution(mesh):
    blocks = P("space", "grp", None, None)
    rows = P("space", "grp", None)
    return jax.shard_map(
        per_device,
        mesh=mesh,
        in_specs=(blocks, blocks, blocks, rows, rows),
        out_specs=(blocks, blocks, blocks),
        check_vma=False,
    )
```

profile of v0, /device:TPU:0, one launch (start us, length us, event | category | flops | bytes accessed | tf_op | source)
XLA Modules:
  0.0 22.2 jit_solution(10372890372090423799)
XLA Ops:
  0.6 20.9 %shard_map.76.in_ref = f32[3,128,128]{2,1,0:T(8,128)S(1)} custom-call(f32[1,1,128,128]{3,2,1,0:T(8,128)} %diag_hbm.1, f32[1,1,128,128]{3,2,1,0:T(8,128)} %x_hbm.1, f32[1,1,128,128]{3,2,1,0:T(8,128)} %y_hbm.1, f32[1,1,128]{2,1,0:T(1,128)} %lev_hbm.1, s32[1,1,2]{2,1,0:T(1,128)} %list_hbm.1), custom_call_target="tpu_custom_call" | custom-call | tf_op jit(solution)/shard_map/pallas_call | solution.py:299
  21.5 0.7 %shard_map.77 = (f32[1,1,128,128]{3,2,1,0:T(8,128)}, f32[1,1,128,128]{3,2,1,0:T(8,128)}, f32[1,1,128,128]{3,2,1,0:T(8,128)}) custom-call(f32[3,128,128]{2,1,0:T(8,128)S(1)} %shard_map.76.in_ref), custom_call_target="tpu_custom_call" | custom-call | tf_op jit(solution)/shard_map/pallas_call | solution.py:333
where the time goes:
time: 22.4 us; the launch traced here: 22.2 us
  Pallas kernels  21.6 us (96%)
  between operations  0.64 us (3%)
    pallas_call x1, Pallas kernels, per_device(): pl.pallas_call(functools.partial(kernel, sizes), out_shape=pltpu.VMEM((3,...  20.9 us
    pallas_call x1, Pallas kernels, per_device(): pl.pallas_call(write_out, out_shape=(block, block, block), in_specs=[vmem...  0.7 us

commit v1 on v0

v1 whole, which is shorter than its diff:
```python
import functools

import jax
import jax.numpy as jnp
from jax import lax
from jax.experimental import pallas as pl
from jax.experimental.pallas import tpu as pltpu
from jax.sharding import PartitionSpec as P

hubbard = 1.0
MESH = pl.DeviceIdType.MESH
F32 = jnp.float32
BF16 = jnp.bfloat16
TILE = 256


def mm(a, b):
    return jnp.dot(a, b, preferred_element_type=F32)


def grid2(rows, cols):
    return (
        lax.broadcasted_iota(jnp.int32, (rows, cols), 0),
        lax.broadcasted_iota(jnp.int32, (rows, cols), 1),
    )


def eye(w):
    r, c = grid2(w, w)
    return r == c


def when(cond, run):
    if cond is True:
        run()
    elif cond is not False:
        pl.when(cond)(run)


def pack(block, ref, flags):
    w = block.shape[0]
    h = w // 2
    r, c = grid2(h, w)
    low = block[h:, :]
    ref[:h, :] = jnp.where((c < h) & (c > r), pltpu.roll(low, h, 1), block[:h, :])
    row = jnp.sum(jnp.where(c == r + h, low, 0.0), axis=0, keepdims=True)
    lane = lax.broadcasted_iota(jnp.int32, (1, w), 1)
    for at, flag in enumerate(flags):
        row = jnp.where(lane == at, flag, row)
    ref[h:, :] = jnp.broadcast_to(row, (8, w))


def unpack(ref):
    w = ref.shape[1]
    h = w // 2
    r, c = grid2(w, w)
    top = ref[:h, :]
    both = jnp.concatenate([top, pltpu.roll(top, h, 1)], axis=0)
    keep = ((r < h) & ((c >= h) | (r >= c))) | ((r >= h) & (c > r))
    block = jnp.where(keep, both, both.T)
    return jnp.where((r == c) & (r >= h), jnp.broadcast_to(ref[h : h + 1, :], (w, w)), block)


def sweep(w, n, a, s, x, rf, emit):
    def bl(i):
        return slice(i * w, (i + 1) * w)

    s[...] = mm(a[...], a[...]).astype(BF16)
    x[0] = mm(a[:w, :], s[...])
    total = jnp.zeros((1, w), F32)
    for step, r0 in enumerate(range(0, n, TILE)):
        r1 = min(r0 + TILE, n)
        f = mm(s[r0:r1, :], s[:, r0:])
        f = jnp.sum(f * f, axis=0, keepdims=True)
        for c0 in range(0, n - r0, w):
            part = f[:, c0 : c0 + w]
            total = total + (part if c0 < r1 - r0 else 2.0 * part)
        if step == 0:
            x[1] = mm(x[0].astype(BF16), s[...])
        if step == 1:
            x[2] = mm(x[1].astype(BF16), s[...])
    x[3] = mm(x[2].astype(BF16), s[...])
    squares = jnp.sum(total, axis=1, keepdims=True)
    scale_two = jnp.sqrt(jnp.sqrt(squares + 1e-06))
    scale_one = jnp.sqrt(scale_two)
    al = 1.5 / scale_one
    be = 0.5 / (scale_one * scale_two)
    coef = [
        -0.75 * al,
        0.75 * be + 0.25 * al * al * al,
        -0.75 * al * al * be,
        0.75 * al * be * be,
        -0.25 * be * be * be,
    ]

    def column(i):
        value = coef[0] * rf[i]
        for p in range(4):
            value = value + coef[1 + p] * x[p, :, bl(i)]
        return value

    emit(column)


def kernel(
    sizes, nb, diag_hbm, x_hbm, y_hbm, lev_hbm, list_hbm, out_ref,
    din, lin, fin, in_sems,
    own, rb1, sp1, rp1, sp2, rp2, rc2, rf3,
    a, s, x, rf, bf, ct1, ct2, tr3,
    send_sems, recv_sems,
):
    nx, ny = sizes
    w = din.shape[0]
    n = (1 + nb) * w
    ix = lax.axis_index("space")
    iy = lax.axis_index("grp")
    lower, upper = jnp.maximum(ix - 1, 0), jnp.minimum(ix + 1, nx - 1)
    has = [ix > 0, ix < nx - 1]
    ups = [False, has[1]]
    downs = [has[0], False]
    dev = [(lower, iy), (upper, iy)]
    opp = [1, 0]
    if nb == 3:
        has += [True]
        ups += [iy == 0]
        downs += [iy == 1]
        dev += [(ix, 1 - iy)]
        opp += [2]
    else:
        has += [iy > 0, iy < ny - 1]
        ups += [False, has[3]]
        downs += [has[2], False]
        dev += [(ix, jnp.maximum(iy - 1, 0)), (ix, jnp.minimum(iy + 1, ny - 1))]
        opp += [3, 2]
    slots = range(nb)
    axis_of = [0, 0, 1, 1]
    coup_hbm = [x_hbm, y_hbm]

    def bl(i):
        return slice(i * w, (i + 1) * w)

    barrier = pltpu.get_barrier_semaphore()
    count = 0
    for k in slots:
        def greet(k=k):
            pl.semaphore_signal(barrier, inc=1, device_id=dev[k], device_id_type=MESH)

        when(has[k], greet)
        count = count + (1 if has[k] is True else has[k].astype(jnp.int32))

    loads = [
        pltpu.make_async_copy(diag_hbm.at[0, 0], din, in_sems.at[0]),
        pltpu.make_async_copy(lev_hbm.at[0], lin, in_sems.at[1]),
        pltpu.make_async_copy(list_hbm.at[0], fin, in_sems.at[2]),
        pltpu.make_async_copy(x_hbm.at[0, 0], own.at[0], in_sems.at[3]),
        pltpu.make_async_copy(y_hbm.at[0, 0], own.at[1], in_sems.at[4]),
    ]
    for load in loads:
        load.start()

    def transfer(kind, k, src, dst):
        return pltpu.make_async_remote_copy(
            src_ref=src, dst_ref=dst.at[opp[k]], send_sem=send_sems.at[kind, k],
            recv_sem=recv_sems.at[kind, opp[k]], device_id=dev[k], device_id_type=MESH,
        )

    def coup1(k):
        return transfer(0, k, coup_hbm[axis_of[k]].at[0, 0], rb1)

    def diag1(k):
        return transfer(1, k, sp1, rp1)

    def coup2(k):
        return transfer(2, k, ct1.at[1 + k], rc2)

    def diag2(k):
        return transfer(3, k, sp2, rp2)

    def coup3(k):
        return transfer(4, k, tr3.at[k], rf3)

    order = list(range(2, nb)) + [1, 0]

    zero = jnp.zeros((w, w), F32)
    for k in slots:
        def clear(k=k):
            rp1[k] = jnp.zeros((w // 2 + 8, w), F32)
            rp2[k] = jnp.zeros((w // 2 + 8, w), F32)
            rc2[k] = zero

        if has[k] is not True:
            when(jnp.logical_not(has[k]), clear)
        if downs[k] is not False:
            def clear_down(k=k):
                rb1[k] = zero

            when(jnp.logical_not(downs[k]), clear_down)
        if ups[k] is not False:
            def clear_up(k=k):
                rf3[k] = zero

            when(jnp.logical_not(ups[k]), clear_up)
    a[...] = jnp.zeros((n, n), BF16)

    pl.semaphore_wait(barrier, count)
    for k in order:
        when(ups[k], lambda k=k: coup1(k).start())
    for load in loads:
        load.wait()

    one_eye = eye(w)
    flags = [
        fin[0, 0].astype(F32) * (ix < nx - 1).astype(F32),
        fin[0, 1].astype(F32) * (iy < ny - 1).astype(F32),
    ]
    raw = din[...]
    onsite = 0.5 * (raw + raw.T) + jnp.where(one_eye, jnp.broadcast_to(lin[...], (w, w)), 0.0)
    pack(onsite, sp1, flags)
    for k in order:
        when(has[k], lambda k=k: diag1(k).start())

    rf[0] = onsite
    a[bl(0), bl(0)] = onsite.astype(BF16)

    def place(k, row, col):
        rf[1 + k] = row
        bf[k] = col
        a[bl(0), bl(1 + k)] = row.astype(BF16)
        a[bl(1 + k), bl(0)] = col.astype(BF16)

    for k in slots:
        if downs[k] is False:
            mine = own[axis_of[k]] * flags[axis_of[k]]
            place(k, mine, mine.T)
    arrival = [1, 0] + list(range(2, nb))
    for k in arrival:
        when(downs[k], lambda k=k: coup1(opp[k]).wait_recv())
        if downs[k] is not False:
            got = rb1[k]
            if ups[k] is not False:
                got = jnp.where(ups[k], own[axis_of[k]], got)
            bf[k] = got
            rf[1 + k] = got.T
    for k in arrival:
        when(has[k], lambda k=k: diag1(opp[k]).wait_recv())
        a[bl(1 + k), bl(1 + k)] = unpack(rp1.at[k]).astype(BF16)
        if downs[k] is not False:
            at = axis_of[k]
            flag = rp1[k, w // 2 : w // 2 + 1, at : at + 1]
            col, row = bf[k], rf[1 + k]
            if ups[k] is not False:
                flag = jnp.where(ups[k], flags[at], flag)
                col, row = jnp.where(ups[k], row, col), jnp.where(ups[k], col, row)
            place(k, row * flag, col * flag)

    def emit_one(column):
        for k in order:
            ct1[1 + k] = column(1 + k)
            when(has[k], lambda k=k: coup2(k).start())
        c0 = column(0)
        two = rf[0] + hubbard * (0.5 * (c0 + c0.T))
        pack(two, sp2, [])
        for k in order:
            when(has[k], lambda k=k: diag2(k).start())
        rf[0] = two
        a[bl(0), bl(0)] = two.astype(BF16)
        for k in slots:
            bf[k] = bf[k] + 0.5 * hubbard * ct1[1 + k].T

    sweep(w, n, a, s, x, rf, emit_one)

    for k in arrival:
        when(has[k], lambda k=k: coup2(opp[k]).wait_recv())
        col = bf[k] + 0.5 * hubbard * rc2[k]
        place(k, col.T, col)
    for k in arrival:
        when(has[k], lambda k=k: diag2(opp[k]).wait_recv())
        a[bl(1 + k), bl(1 + k)] = unpack(rp2.at[k]).astype(BF16)

    halves = [None, None]

    def emit_two(column):
        for k in order:
            ct = column(1 + k)
            if downs[k] is not False:
                tr3[k] = ct.T
                when(downs[k], lambda k=k: coup3(k).start())
            if ups[k] is not False:
                half = 0.5 * ct
                if downs[k] is not False:
                    half = jnp.where(ups[k], half, 0.0)
                out_ref[1 + axis_of[k]] = half
        c0 = column(0)
        out_ref[0] = 0.5 * (c0 + c0.T) + jnp.where(one_eye, 0.5, 0.0)

    sweep(w, n, a, s, x, rf, emit_two)

    for k in reversed(order):
        if ups[k] is not False:
            when(ups[k], lambda k=k: coup3(opp[k]).wait_recv())
            out_ref[1 + axis_of[k]] = out_ref[1 + axis_of[k]] + 0.5 * rf3[k]
    for k in slots:
        def drain(k=k):
            diag1(k).wait_send()
            coup2(k).wait_send()
            diag2(k).wait_send()

        when(has[k], drain)
        when(ups[k], lambda k=k: coup1(k).wait_send())
        when(downs[k], lambda k=k: coup3(k).wait_send())


def write_out(in_ref, od_ref, ox_ref, oy_ref, sems):
    copies = [
        pltpu.make_async_copy(in_ref.at[i], ref.at[0, 0], sems.at[i])
        for i, ref in enumerate((od_ref, ox_ref, oy_ref))
    ]
    for copy in copies:
        copy.start()
    for copy in copies:
        copy.wait()


def per_device(diag_blocks, x_coupling, y_coupling, levels, listed):
    w = diag_blocks.shape[-1]
    sizes = (lax.axis_size("space"), lax.axis_size("grp"))
    nb = 3 if sizes[1] == 2 else 4
    n = (1 + nb) * w
    block = jax.ShapeDtypeStruct((1, 1, w, w), F32)
    any_spec = pl.BlockSpec(memory_space=pl.ANY)
    vmem_spec = pl.BlockSpec(memory_space=pltpu.VMEM)
    half = w // 2 + 8
    results = pl.pallas_call(
        functools.partial(kernel, sizes, nb),
        out_shape=pltpu.VMEM((3, w, w), F32),
        in_specs=[any_spec] * 5,
        out_specs=vmem_spec,
        scratch_shapes=[
            pltpu.VMEM((w, w), F32),
            pltpu.VMEM((1, w), F32),
            pltpu.SMEM((1, 2), jnp.int32),
            pltpu.SemaphoreType.DMA((5,)),
            pltpu.VMEM((2, w, w), F32),
            pltpu.VMEM((nb, w, w), F32),
            pltpu.VMEM((half, w), F32),
            pltpu.VMEM((nb, half, w), F32),
            pltpu.VMEM((half, w), F32),
            pltpu.VMEM((nb, half, w), F32),
            pltpu.VMEM((nb, w, w), F32),
            pltpu.VMEM((nb, w, w), F32),
            pltpu.VMEM((n, n), BF16),
            pltpu.VMEM((n, n), BF16),
            pltpu.VMEM((4, w, n), F32),
            pltpu.VMEM((1 + nb, w, w), F32),
            pltpu.VMEM((nb, w, w), F32),
            pltpu.VMEM((1 + nb, w, w), F32),
            pltpu.VMEM((1 + nb, w, w), F32),
            pltpu.VMEM((nb, w, w), F32),
            pltpu.SemaphoreType.DMA((5, nb)),
            pltpu.SemaphoreType.DMA((5, nb)),
        ],
        compiler_params=pltpu.CompilerParams(collective_id=0, has_side_effects=True),
    )(diag_blocks, x_coupling, y_coupling, levels, listed)
    return pl.pallas_call(
        write_out,
        out_shape=(block, block, block),
        in_specs=[vmem_spec],
        out_specs=(any_spec,) * 3,
        scratch_shapes=[pltpu.SemaphoreType.DMA((3,))],
    )(pltpu.with_memory_space_constraint(results, pltpu.VMEM))


def solution(mesh):
    blocks = P("space", "grp", None, None)
    rows = P("space", "grp", None)
    return jax.shard_map(
        per_device,
        mesh=mesh,
        in_specs=(blocks, blocks, blocks, rows, rows),
        out_specs=(blocks, blocks, blocks),
        check_vma=False,
    )
```

time: 22.4 us -> 18.9 us (0.84)
  Pallas kernels: 21.6 us -> 18.2 us
    pallas_call x1, Pallas kernels: 20.9 us -> 17.5 us  [per_device(): pl.pallas_call(functools.partial(kernel, sizes, nb), out_shape=pltpu.VMEM...]
where the time goes in v1:
time: 18.9 us; the launch traced here: 18.8 us
  Pallas kernels  18.2 us (96%)
  between operations  0.64 us (3%)
    pallas_call x1, Pallas kernels, per_device(): pl.pallas_call(functools.partial(kernel, sizes, nb), out_shape=pltpu.VMEM...  17.5 us
    pallas_call x1, Pallas kernels, per_device(): pl.pallas_call(write_out, out_shape=(block, block, block), in_specs=[vmem...  0.7 us

profile of v1, /device:TPU:0, one launch (start us, length us, event | category | flops | bytes accessed | tf_op | source)
XLA Modules:
  0.0 18.8 jit_solution(2063987534039006869)
XLA Ops:
  0.6 17.5 %shard_map.76.in_ref = f32[3,128,128]{2,1,0:T(8,128)S(1)} custom-call(f32[1,1,128,128]{3,2,1,0:T(8,128)} %diag_hbm.1, f32[1,1,128,128]{3,2,1,0:T(8,128)} %x_hbm.1, f32[1,1,128,128]{3,2,1,0:T(8,128)} %y_hbm.1, f32[1,1,128]{2,1,0:T(1,128)} %lev_hbm.1, s32[1,1,2]{2,1,0:T(1,128)} %list_hbm.1), custom_call_target="tpu_custom_call" | custom-call | tf_op jit(solution)/shard_map/pallas_call | solution.py:333
  18.1 0.7 %shard_map.77 = (f32[1,1,128,128]{3,2,1,0:T(8,128)}, f32[1,1,128,128]{3,2,1,0:T(8,128)}, f32[1,1,128,128]{3,2,1,0:T(8,128)}) custom-call(f32[3,128,128]{2,1,0:T(8,128)S(1)} %shard_map.76.in_ref), custom_call_target="tpu_custom_call" | custom-call | tf_op jit(solution)/shard_map/pallas_call | solution.py:364
